TPU v7x, 256 devices: a whole 4x4x8 slice. The times are simulated.
256 devices in a mesh: dp: 128 (over x_lo, z, y, core), space: 2 (over x_hi).
Axes of the slice: x: 4 (x_hi: 2, x_lo: 2; x = x_hi * 2 + x_lo), y: 4, z: 8, core: 2. Of those that a mesh axis runs over, the one named last changes fastest.
Arguments:
- feature_map: bfloat16 [128, 24, 84, 256], P('dp', 'space'), may hold values from -6 to 6
- proposals: int32 [128, 128, 4], P('dp'), may hold values from 0 to 84, as said below
- hidden_weight: bfloat16 [12544, 512], P(None, 'space'), may hold values from -0.0546875 to 0.0546875
- output_weight: bfloat16 [512, 512], P('space'), may hold values from -0.25 to 0.25
- upstream: bfloat16 [128, 128, 512], P('dp'), may hold values from -6 to 6
Outputs:
- hidden_weight_grad: float32 [12544, 512], P('dp', 'space')
- output_weight_grad: float32 [512, 512], P('space')
- feature_grad: float32 [128, 24, 84, 256], P('dp', 'space')
Inputs may be any that keep to these rules, and one draw needn't show every extreme that they name: `proposals`: each row holds top, left, bottom, right with top < bottom <= 24 and left < right <= 84.
All inputs are finite; a program needn't handle non-finite values.
Results may differ from a plain program's by a relative error of at most 0.012.
Values may be sent and summed in bfloat16 or wider, within the bound.
A program may use at most 128 MiB of HBM per device.

v0:
```python
import jax
import jax.numpy as jnp
from jax import lax
from jax.sharding import PartitionSpec as P

POOL = 7


def copy_for_each(x, axis):
    size = lax.axis_size(axis)
    return lax.all_to_all(jnp.broadcast_to(x[None], (size, *x.shape)), axis, 0, 0, tiled=True)


def joined_along(blocks, dim):
    blocks = jnp.moveaxis(blocks, 0, dim)
    dims = blocks.shape
    return blocks.reshape(*dims[:dim], dims[dim] * dims[dim + 1], *dims[dim + 2 :])


def collect(x, axis, dim):
    blocks = copy_for_each(x, axis)
    return joined_along(blocks, dim)


def over_copies(x, axis):
    return copy_for_each(x, axis).astype(jnp.float32).sum(axis=0)


def in_blocks(x, dim, size):
    before, after = (x.shape[:dim], x.shape[dim + 1 :])
    return jnp.moveaxis(x.reshape(*before, size, -1, *after), dim, 0)


def summed_on_arrival(x, axis, dim):
    blocks = in_blocks(x, dim, lax.axis_size(axis))
    arrived = lax.all_to_all(blocks, axis, split_axis=0, concat_axis=0, tiled=True)
    return arrived.astype(jnp.float32).sum(axis=0)


def axis_weights(low_edge, high_edge, grid_points):
    edge_start = low_edge.astype(jnp.float32)
    bin_size = (high_edge - low_edge).astype(jnp.float32) / POOL
    bin_index = jnp.arange(POOL).astype(jnp.float32)
    offsets = jnp.array([0.25, 0.75], jnp.float32)
    sample_points = (
        edge_start[:, None, None]
        + (bin_index[None, :, None] + offsets[None, None, :]) * bin_size[:, None, None]
        - 0.5
    )
    weights = jnp.maximum(
        0.0, 1.0 - jnp.abs(sample_points[..., None] - grid_points[None, None, None, :])
    )
    return jnp.mean(weights, axis=2)


def activate(values):
    return jax.nn.gelu(values, approximate=True)


def gelu_grad(values, incoming):
    return jax.vjp(activate, values)[1](incoming)[0]


def block_shape(proposal_count):
    block_size = 32
    return (block_size, proposal_count // block_size)


def crop_rows(own_map, row_weight, col_weight):
    height_cells, width_cells, channels = own_map.shape
    proposal_count = row_weight.shape[0]
    block_size, block_count = block_shape(proposal_count)
    flattened = jnp.transpose(own_map, (1, 0, 2)).reshape(width_cells, height_cells * channels)

    def per_block(blocks):
        row_part, col_part = blocks
        across = jnp.dot(
            col_part.reshape(block_size * POOL, width_cells),
            flattened,
            preferred_element_type=jnp.float32,
        )
        across = across.reshape(block_size, POOL, height_cells, channels)
        return jnp.einsum("riy,rjyc->rijc", row_part, across, precision=lax.Precision.HIGHEST)

    pooled = lax.map(
        per_block,
        (
            row_weight.reshape(block_count, block_size, POOL, height_cells),
            col_weight.reshape(block_count, block_size, POOL, width_cells),
        ),
    )
    return pooled.reshape(proposal_count, POOL * POOL * channels)


def crop_back(grad_pooled, row_weight, col_weight, channels):
    proposal_count, _, height_cells = row_weight.shape
    width_cells = col_weight.shape[2]
    block_size, block_count = block_shape(proposal_count)

    def per_block(running, blocks):
        row_part, col_part, grad_part = blocks
        grad_block = grad_part.reshape(block_size, POOL, POOL, channels)
        spread = jnp.einsum("riy,rijc->rjyc", row_part, grad_block, precision=lax.Precision.HIGHEST)
        added = lax.dot_general(
            col_part.astype(jnp.float32).reshape(block_size * POOL, width_cells),
            spread.reshape(block_size * POOL, height_cells * channels),
            (((0,), (0,)), ((), ())),
            precision=lax.Precision.HIGHEST,
            preferred_element_type=jnp.float32,
        )
        return (running + added, None)

    start = jnp.zeros((width_cells, height_cells * channels), jnp.float32)
    blocks = (
        row_weight.reshape(block_count, block_size, POOL, height_cells),
        col_weight.reshape(block_count, block_size, POOL, width_cells),
        grad_pooled.reshape(block_count, block_size, grad_pooled.shape[1]),
    )
    total, _ = lax.scan(per_block, start, blocks)
    return jnp.transpose(total.reshape(width_cells, height_cells, channels), (1, 0, 2))


def on_device(feature_map, proposals, hidden_weight, output_weight, upstream):
    own_map = feature_map[0]
    corners = proposals[0]
    own_height = own_map.shape[0]
    map_width = own_map.shape[1]
    channels = own_map.shape[2]
    col_weight = axis_weights(
        corners[:, 1], corners[:, 3], jnp.arange(map_width, dtype=jnp.int32).astype(jnp.float32)
    ).astype(jnp.bfloat16)
    full_grid = jnp.arange(own_height * lax.axis_size("space"), dtype=jnp.int32).astype(jnp.float32)
    full_weight = axis_weights(corners[:, 0], corners[:, 2], full_grid)
    whole_map = collect(own_map, "space", 0)
    pooled = crop_rows(whole_map, full_weight, col_weight).astype(jnp.bfloat16)
    pre_hidden = jnp.dot(pooled, hidden_weight, preferred_element_type=jnp.float32)
    hidden = activate(pre_hidden).astype(jnp.bfloat16)
    pre_output = over_copies(
        jnp.dot(hidden, output_weight, preferred_element_type=jnp.float32).astype(jnp.bfloat16),
        "space",
    ).astype(jnp.float32)
    output_delta = gelu_grad(pre_output, upstream[0].astype(jnp.float32)).astype(jnp.bfloat16)
    step_second = lax.dot_general(
        hidden, output_delta, (((0,), (0,)), ((), ())), preferred_element_type=jnp.float32
    )
    second_total = lax.psum(step_second, "dp")
    hidden_back = lax.dot_general(
        output_delta, output_weight, (((1,), (1,)), ((), ())), preferred_element_type=jnp.float32
    )
    hidden_delta = gelu_grad(pre_hidden, hidden_back).astype(jnp.bfloat16)
    step_first = lax.dot_general(
        pooled, hidden_delta, (((0,), (0,)), ((), ())), preferred_element_type=jnp.float32
    )
    first_total = lax.psum_scatter(step_first, "dp", scatter_dimension=0, tiled=True)
    partial_grad = lax.dot_general(
        hidden_delta, hidden_weight, (((1,), (1,)), ((), ())), preferred_element_type=jnp.float32
    )
    whole_grad = crop_back(partial_grad, full_weight, col_weight, channels)
    map_grad = summed_on_arrival(whole_grad.astype(jnp.bfloat16), "space", 0)
    return (first_total, second_total, map_grad[None])


def solution(mesh):
    placed = (
        P("dp", "space", None, None),
        P("dp", None, None),
        P(None, "space"),
        P("space", None),
        P("dp", None, None),
    )
    return jax.shard_map(
        on_device,
        mesh=mesh,
        in_specs=placed,
        out_specs=(P("dp", "space"), P("space", None), P("dp", "space", None, None)),
        check_vma=False,
    )
```

profile of v0, /device:TPU:6, one launch (start us, length us, event | category | flops | bytes accessed | tf_op | source)
XLA Modules:
  0.0 1236.6 jit_solution(13362167307446305481)
XLA Ops:
  9.4 5.0 all-to-all-start
  16.5 10.3 all-to-all-done
  27.4 34.8 %while.21 = (s32[]{:T(128)}, bf16[4,32,7,7,256]{4,2,3,1,0:T(8,128)(2,1)}, f32[4,32,7,24]{3,2,1,0:T(8,128)S(1)}, bf16[4,32,7,84]{3,1,0,2:T(8,128)(2,1)S(1)}, bf16[84,6144]{1,0:T(8,128)(2,1)S(1)}, /*index=5*/s32[]{:T(128)}) while((s32[]{:T(128)}, bf16[4,32,7,7,256]{4,2,3,1,0:T(8,128)(2,1)}, f32[4,32,7,24]{3,2,1,0:T(8,128)S(1)}, ...), condition=%wide.region_3.4_spmd, body=%wide.region_2.3_spmd.sunk | while | flops 346816512 | bytes 18293832 | solution.py:85
  28.7 7.5 bitcast_dynamic-update-slice_fusion.2
  37.4 7.5 bitcast_dynamic-update-slice_fusion.2
  46.0 7.5 bitcast_dynamic-update-slice_fusion.2
  54.7 7.4 bitcast_dynamic-update-slice_fusion.2
  62.9 5.2 copy.44
  68.1 5.6 convert_element_type.119
  79.1 7.3 all-to-all-start.1
  93.5 6.5 fusion.38
  106.0 91.8 %while.22 = (s32[]{:T(128)}, f32[84,6144]{1,0:T(8,128)}, bf16[4,32,7,84]{3,2,1,0:T(8,128)(2,1)}, f32[4,32,12544]{2,1,0:T(8,128)}, f32[4,32,7,24]{3,2,1,0:T(8,128)}, /*index=5*/s32[]{:T(128)}, s32[]{:T(128)}) while((s32[]{:T(128)}, f32[84,6144]{1,0:T(8,128)}, bf16[4,32,7,84]{3,2,1,0:T(8,128)(2,1)}, f32[4,32,12544]{2,1,0:T(8,128)}, ...), condition=%wide.region_8.9_spmd.clone, body=%wide.region_7.8_spmd.clone.sunk | while | flops 1503903744 | bytes 51011988 | solution.py:119
  110.4 5.7 fusion.71
  121.6 5.9 convolution_add_fusion.2
  133.4 5.7 fusion.71
  144.6 5.9 convolution_add_fusion.2
  156.3 5.7 fusion.71
  167.5 5.9 convolution_add_fusion.2
  179.3 5.7 fusion.71
  190.5 5.9 convolution_add_fusion.2
  201.0 6.9 all-to-all-start.2
  208.6 328.2 %fusion = f32[104,256]{1,0:T(8,128)S(1)} fusion(f32[12544,256]{1,0:T(8,128)} %fusion.38), kind=kCustom, calls=%all-reduce-scatter | all-reduce-scatter fusion | flops 3407873 | bytes 12952576
  558.7 5.1 collective-permute-done.5
  567.8 660.0 %all-reduce.4.cloned.1.call-done = f32[256,512]{1,0:T(8,128)} async-done(((f32[256,512]{1,0:T(8,128)}), f32[256,512]{1,0:T(8,128)}) %all-reduce.4.cloned.1.call-update) | async-done | bytes 524304 | tf_op jit(solution)/shard_map/psum | solution.py:146
  (129 shorter events, 104.8 us)
Async XLA Ops:
  7.2 71.0 %copy-start = (bf16[256,512]{1,0:T(8,128)(2,1)S(1)}, bf16[256,512]{1,0:T(8,128)(2,1)}, u32[]{:S(2)}) copy-start(bf16[256,512]{1,0:T(8,128)(2,1)} %param.14) | copy-start | bytes 786436
  7.2 7.2 copy-start.9
  7.2 7.2 copy-start.8
  9.4 17.5 %all-to-all-start = ((bf16[2,12,84,256]{3,2,1,0:T(8,128)(2,1)}), bf16[2,12,84,256]{3,2,1,0:T(8,128)(2,1)S(1)}, u32[]{:S(2)}, u32[]{:S(2)}) async-start(bf16[2,12,84,256]{3,2,1,0:T(8,128)(2,1)} %broadcast_in_dim.17), calls=%async_computation | async-start | bytes 2162688 | tf_op jit(solution)/shard_map/all_to_all | solution.py:11
  79.1 10.8 all-to-all-start.1
  89.9 10.1 slice-start
  93.5 6.5 slice-start.1
  100.0 4.9 copy-start.7
  116.2 5.5 copy-start.2
  139.1 5.5 copy-start.2
  162.1 5.5 copy-start.2
  185.0 5.5 copy-start.2
  201.0 365.0 %all-to-all-start.2 = ((bf16[2,12,84,256]{3,2,1,0:T(8,128)(2,1)}), bf16[2,12,84,256]{3,2,1,0:T(8,128)(2,1)S(1)}, u32[]{:S(2)}, u32[]{:S(2)}) async-start(bf16[2,12,84,256]{3,2,1,0:T(8,128)(2,1)} %bitcast.23), calls=%async_computation.2 | async-start | bytes 2162688 | tf_op jit(solution)/shard_map/all_to_all | solution.py:36
  207.9 1020.0 %all-reduce.4.cloned.1.call-start = ((), (), s32[]{:S(2)}) async-start(), calls=%async_computation.3 | async-start | bytes 1048576 | tf_op jit(solution)/shard_map/psum | solution.py:146
  208.6 348.9 %copy-start.10 = (u32[256]{0:T(256)S(1)}, u32[256]{0:T(256)}, u32[]{:S(2)}) copy-start(u32[256]{0:T(256)} %constant.68) | copy-start | bytes 3076
  536.8 16.5 %collective-permute-start = (f32[104,256]{1,0:T(8,128)S(1)}, f32[104,256]{1,0:T(8,128)S(1)}, u32[]{:S(2)}, u32[]{:S(2)}) collective-permute-start(f32[104,256]{1,0:T(8,128)S(1)} %fusion), channel_id=1, source_target_pairs={{0,2},{2,4},{4,6},{6,8},{8,10},{10,12},{12,14},{14,16},{16,18},{18... | collective-permute-start | bytes 319496
  538.8 16.7 %collective-permute-start.1 = (f32[104,256]{1,0:T(8,128)S(1)}, f32[104,256]{1,0:T(8,128)S(1)}, u32[]{:S(2)}, u32[]{:S(2)}) collective-permute-start(f32[104,256]{1,0:T(8,128)S(1)} %fusion), channel_id=1, source_target_pairs={{0,4},{2,6},{4,8},{6,10},{8,12},{10,14},{12,16},{14,18},{16,20},{1... | collective-permute-start | bytes 319496
  540.7 8.0 collective-permute-start.7
  542.6 16.1 %collective-permute-start.2 = (f32[104,256]{1,0:T(8,128)S(1)}, f32[104,256]{1,0:T(8,128)S(1)}, u32[]{:S(2)}, u32[]{:S(2)}) collective-permute-start(f32[104,256]{1,0:T(8,128)S(1)} %fusion), channel_id=1, source_target_pairs={{0,6},{2,8},{4,10},{6,12},{8,14},{10,16},{12,18},{14,20},{16,22},{... | collective-permute-start | bytes 319496
  544.6 14.1 %collective-permute-start.3 = (f32[104,256]{1,0:T(8,128)S(1)}, f32[104,256]{1,0:T(8,128)S(1)}, u32[]{:S(2)}, u32[]{:S(2)}) collective-permute-start(f32[104,256]{1,0:T(8,128)S(1)} %fusion), channel_id=1, source_target_pairs={{0,8},{2,10},{4,12},{6,14},{8,16},{10,18},{12,20},{14,22},{16,24},... | collective-permute-start | bytes 319496
  548.7 10.0 collective-permute-start.4
  553.3 10.5 collective-permute-start.5
  555.5 8.3 collective-permute-start.6
  563.8 665.9 %copy-start.1 = (bf16[256,512]{1,0:T(8,128)(2,1)S(1)}, bf16[256,512]{1,0:T(8,128)(2,1)}, u32[]{:S(2)}) copy-start(bf16[256,512]{1,0:T(8,128)(2,1)} %param.14) | copy-start | bytes 786436
  (7 other events, 7.8 us)
Sparse Core Ops, SparseCore 0:
  211.9 1015.9 all-reduce.3
where the time goes:
time: 1240 us
  waiting for transfers between devices  680 us (55%)
  blocking collectives  328 us (26%)
  matrix products  97.2 us (8%)
  local copies, waits for them, and re-layouts  72.5 us (6%)
  starting transfers between devices  37.5 us (3%)
  between operations  15 us (1%)
    psum x1, waiting for transfers between devices, on_device(): second_total = lax.psum(step_second, 'dp')  660 us
    unnamed x1, blocking collectives  328 us
    dot_general x4, matrix products, per_block(): jnp.einsum('riy,rjyc->rijc', row_part, across, precision=lax.Precision.HI...  29.8 us
    while x24, local copies, waits for them, and re-layouts  24.8 us
  transfers between devices with their start and end apart: 12, of which 5 were waited for; matrix products, arithmetic and copies ran while one was open for 27% of the time, Pallas kernels for 0%

commit v1 on v0

--- a/solution.py
+++ b/solution.py
@@ -143,7 +143,7 @@
     step_second = lax.dot_general(
         hidden, output_delta, (((0,), (0,)), ((), ())), preferred_element_type=jnp.float32
     )
-    second_total = lax.psum(step_second, "dp")
+    second_total = jnp.sum(lax.all_gather(step_second, "dp"), axis=0)
     hidden_back = lax.dot_general(
         output_delta, output_weight, (((1,), (1,)), ((), ())), preferred_element_type=jnp.float32
     )

time: 1240 us -> 610 us (0.49)
  waiting for transfers between devices: 680 us -> 19.9 us
  other arithmetic: 5.65 us -> 26.6 us
  blocking collectives: 328 us -> 343 us
    psum x1 -> x0, waiting for transfers between devices: 660 us -> none  [on_device(): second_total = lax.psum(step_second, 'dp')]
    reduce_sum x0 -> x1, other arithmetic: none -> 21.7 us  [on_device(): second_total = jnp.sum(lax.all_gather(step_second, 'dp'), axis=0)]
    while x24 -> x40, local copies, waits for them, and re-layouts: 24.8 us -> 36.2 us
  transfers between devices with their start and end apart: 12 -> 11, of which waited for: 5 -> 5; matrix products, arithmetic and copies ran while one was open for 27% -> 73% of each run, Pallas kernels for 0% -> 0%
where the time goes in v1:
time: 610 us; the launch traced here: 609 us
  blocking collectives  343 us (56%)
  matrix products  97.9 us (16%)
  local copies, waits for them, and re-layouts  75.4 us (12%)
  starting transfers between devices  29.9 us (5%)
  other arithmetic  26.6 us (4%)
  waiting for transfers between devices  19.9 us (3%)
  between operations  15.1 us (2%)
    unnamed x1, blocking collectives  334 us
    while x40, local copies, waits for them, and re-layouts  36.2 us
    dot_general x4, matrix products, per_block(): jnp.einsum('riy,rjyc->rijc', row_part, across, precision=lax.Precision.HI...  26.1 us
    dot_general x4, matrix products, per_block(): lax.dot_general(col_part.astype(jnp.float32).reshape(block_size * POOL, w...  23.9 us
    dot_general x4, matrix products, per_block(): jnp.einsum('riy,rijc->rjyc', row_part, grad_block, precision=lax.Precisio...  22.9 us
    reduce_sum x1, other arithmetic, on_device(): second_total = jnp.sum(lax.all_gather(step_second, 'dp'), axis=0)  21.7 us
    unnamed x8, starting transfers between devices  16.8 us
  transfers between devices with their start and end apart: 11, of which 5 were waited for; matrix products, arithmetic and copies ran while one was open for 73% of the time, Pallas kernels for 0%

profile of v1, /device:TPU:6, one launch (start us, length us, event | category | flops | bytes accessed | tf_op | source)
XLA Modules:
  0.0 608.5 jit_solution(911998769442499711)
XLA Ops:
  16.2 10.6 %all-to-all-done = bf16[2,12,84,256]{3,2,1,0:T(8,128)(2,1)S(1)} async-done(((bf16[2,12,84,256]{3,2,1,0:T(8,128)(2,1)}), bf16[2,12,84,256]{3,2,1,0:T(8,128)(2,1)S(1)}, u32[]{:S(2)}, u32[]{:S(2)}) %all-to-all-start) | async-done | bytes 1032224 | tf_op jit(solution)/shard_map/all_to_all | solution.py:11
  27.4 42.8 %while.21 = (s32[]{:T(128)}, bf16[4,32,7,7,256]{4,2,3,1,0:T(8,128)(2,1)}, f32[4,32,7,24]{3,2,1,0:T(8,128)S(1)}, bf16[4,32,7,84]{3,1,0,2:T(8,128)(2,1)S(1)}, bf16[84,6144]{1,0:T(8,128)(2,1)S(1)}, /*index=5*/s32[]{:T(128)}) while((s32[]{:T(128)}, bf16[4,32,7,7,256]{4,2,3,1,0:T(8,128)(2,1)}, f32[4,32,7,24]{3,2,1,0:T(8,128)S(1)}, ...), condition=%wide.region_3.4_spmd, body=%wide.region_2.3_spmd.sunk | while | flops 346816512 | bytes 43984008 | solution.py:85
  29.9 6.5 %bitcast_dynamic-update-slice_fusion.2 = bf16[4,32,7,7,256]{4,2,3,1,0:T(8,128)(2,1)S(1)} fusion(bf16[4,32,7,7,256]{4,2,3,1,0:T(8,128)(2,1)S(1)} %copy-done.7, s32[]{:T(128)S(6)} %copy.81, f32[32,7,24,256]{3,0,2,1:T(8,128)S(1)} %fusion.66, f32[4,32,7,24]{3,2,1,0:T(8,128)S(1)} %get-tuple-element.209), kind=kOutput, calls=%fused_computation.2.clone.1 | convolution fusion | flops 115605504 | bytes 7472128 | tf_op jit(solution)/shard_map/while/body/eval_jaxpr/riy,rjyc->rijc/dot_general | solution.py:83
  40.6 6.5 %bitcast_dynamic-update-slice_fusion.2 = bf16[4,32,7,7,256]{4,2,3,1,0:T(8,128)(2,1)S(1)} fusion(bf16[4,32,7,7,256]{4,2,3,1,0:T(8,128)(2,1)S(1)} %copy-done.7, s32[]{:T(128)S(6)} %copy.81, f32[32,7,24,256]{3,0,2,1:T(8,128)S(1)} %fusion.66, f32[4,32,7,24]{3,2,1,0:T(8,128)S(1)} %get-tuple-element.209), kind=kOutput, calls=%fused_computation.2.clone.1 | convolution fusion | flops 115605504 | bytes 7472128 | tf_op jit(solution)/shard_map/while/body/eval_jaxpr/riy,rjyc->rijc/dot_general | solution.py:83
  51.2 6.5 %bitcast_dynamic-update-slice_fusion.2 = bf16[4,32,7,7,256]{4,2,3,1,0:T(8,128)(2,1)S(1)} fusion(bf16[4,32,7,7,256]{4,2,3,1,0:T(8,128)(2,1)S(1)} %copy-done.7, s32[]{:T(128)S(6)} %copy.81, f32[32,7,24,256]{3,0,2,1:T(8,128)S(1)} %fusion.66, f32[4,32,7,24]{3,2,1,0:T(8,128)S(1)} %get-tuple-element.209), kind=kOutput, calls=%fused_computation.2.clone.1 | convolution fusion | flops 115605504 | bytes 7472128 | tf_op jit(solution)/shard_map/while/body/eval_jaxpr/riy,rjyc->rijc/dot_general | solution.py:83
  61.9 6.5 %bitcast_dynamic-update-slice_fusion.2 = bf16[4,32,7,7,256]{4,2,3,1,0:T(8,128)(2,1)S(1)} fusion(bf16[4,32,7,7,256]{4,2,3,1,0:T(8,128)(2,1)S(1)} %copy-done.7, s32[]{:T(128)S(6)} %copy.81, f32[32,7,24,256]{3,0,2,1:T(8,128)S(1)} %fusion.66, f32[4,32,7,24]{3,2,1,0:T(8,128)S(1)} %get-tuple-element.209), kind=kOutput, calls=%fused_computation.2.clone.1 | convolution fusion | flops 115605504 | bytes 7472128 | tf_op jit(solution)/shard_map/while/body/eval_jaxpr/riy,rjyc->rijc/dot_general | solution.py:83
  71.0 5.2 copy.44
  76.2 5.6 convert_element_type.119
  81.8 5.0 fusion.37
  87.1 8.9 %all_to_all.15 = bf16[2,128,512]{2,1,0:T(8,128)(2,1)S(1)} all-to-all(bf16[2,128,512]{2,1,0:T(8,128)(2,1)S(1)} %broadcast_in_dim.19), channel_id=1, replica_groups=mesh['dp'=128,'space'=2] {'space'}, dimensions={0} | all-to-all | bytes 524288 | tf_op jit(solution)/shard_map/all_to_all | solution.py:11
  98.7 7.8 %fusion.39 = f32[128,12544]{1,0:T(8,128)} fusion(bf16[128,256]{1,0:T(8,128)(2,1)S(1)} %fusion.35, bf16[12544,256]{1,0:T(8,128)(2,1)} %param.13), kind=kOutput, calls=%fused_computation.67 | convolution fusion | flops 822083584 | bytes 12910592 | tf_op jit(solution)/shard_map/dot_general | solution.py:155
  106.5 88.6 %while.22 = (s32[]{:T(128)}, f32[84,6144]{1,0:T(8,128)}, bf16[4,32,7,84]{3,2,1,0:T(8,128)(2,1)S(1)}, f32[4,32,12544]{2,1,0:T(8,128)}, f32[4,32,7,24]{3,2,1,0:T(8,128)}, /*index=5*/s32[]{:T(128)}, s32[]{:T(128)}) while((s32[]{:T(128)}, f32[84,6144]{1,0:T(8,128)}, bf16[4,32,7,84]{3,2,1,0:T(8,128)(2,1)S(1)}, ...), condition=%wide.region_8.9_spmd.clone, body=%wide.region_7.8_spmd.clone.sunk | while | flops 1503903744 | bytes 51011488 | solution.py:119
  111.0 5.7 fusion.71
  121.3 6.0 convolution_add_fusion.2
  133.2 5.7 fusion.71
  143.4 6.0 convolution_add_fusion.2
  155.3 5.7 fusion.71
  165.6 6.0 convolution_add_fusion.2
  177.5 5.7 fusion.71
  187.7 6.0 convolution_add_fusion.2
  198.4 8.1 %all-to-all-start.2 = ((bf16[2,12,84,256]{3,2,1,0:T(8,128)(2,1)}), bf16[2,12,84,256]{3,2,1,0:T(8,128)(2,1)}, u32[]{:S(2)}, u32[]{:S(2)}) async-start(bf16[2,12,84,256]{3,2,1,0:T(8,128)(2,1)} %bitcast.113), calls=%async_computation.2 | async-start | bytes 2162688 | tf_op jit(solution)/shard_map/all_to_all | solution.py:36
  206.4 6.5 %fusion.38 = f32[12544,256]{1,0:T(8,128)} fusion(bf16[128,12544]{1,0:T(8,128)(2,1)S(1)} %copy-done.5, bf16[128,256]{1,0:T(8,128)(2,1)S(1)} %fusion.35), kind=kOutput, calls=%fused_computation.66 | convolution fusion | flops 822083584 | bytes 16121856 | tf_op jit(solution)/shard_map/dot_general | solution.py:151
  212.9 334.3 %fusion = f32[104,256]{1,0:T(8,128)S(1)} fusion(f32[12544,256]{1,0:T(8,128)} %fusion.38), kind=kCustom, calls=%all-reduce-scatter | all-reduce-scatter fusion | flops 3407873 | bytes 12952576
  580.0 21.7 %reduce_sum.48 = f32[256,512]{1,0:T(8,128)} reduce(f32[128,256,512]{2,1,0:T(8,128)} %bitcast.20, f32[]{:T(128)} %constant.24.clone.1), dimensions={0}, to_apply=%region_6.7 | reduce | flops 16646144 | bytes 67633152 | tf_op jit(solution)/shard_map/reduce_sum | solution.py:146
  (145 shorter events, 106.5 us)
Async XLA Ops:
  7.2 79.7 %copy-start = (bf16[256,512]{1,0:T(8,128)(2,1)S(1)}, bf16[256,512]{1,0:T(8,128)(2,1)}, u32[]{:S(2)}) copy-start(bf16[256,512]{1,0:T(8,128)(2,1)} %param.14) | copy-start | bytes 786436
  7.2 7.2 %copy-start.14 = (f32[2]{0:T(128)S(1)}, f32[2]{0:T(128)}, u32[]{:S(2)}) copy-start(f32[2]{0:T(128)} %constant.62.clone) | copy-start | bytes 28
  7.2 7.2 %copy-start.13 = (s32[1,128,4]{1,2,0:T(4,128)S(1)}, s32[1,128,4]{1,2,0:T(4,128)}, u32[]{:S(2)}) copy-start(s32[1,128,4]{1,2,0:T(4,128)} %param.12) | copy-start | bytes 6148
  9.4 17.5 %all-to-all-start = ((bf16[2,12,84,256]{3,2,1,0:T(8,128)(2,1)}), bf16[2,12,84,256]{3,2,1,0:T(8,128)(2,1)S(1)}, u32[]{:S(2)}, u32[]{:S(2)}) async-start(bf16[2,12,84,256]{3,2,1,0:T(8,128)(2,1)} %broadcast_in_dim.17), calls=%async_computation | async-start | bytes 2162688 | tf_op jit(solution)/shard_map/all_to_all | solution.py:11
  14.3 565.6 %all-gather.3.cloned.1.call-start = ((), (), s32[]{:S(2)}) async-start(), calls=%async_computation.3 | async-start | bytes 67633152 | tf_op jit(solution)/shard_map/all_gather | solution.py:146
  16.0 11.4 %copy-start.9 = (bf16[128,7,84]{0,2,1:T(8,128)(2,1)}, bf16[128,7,84]{0,2,1:T(8,128)(2,1)S(1)}, u32[]{:S(2)}) copy-start(bf16[128,7,84]{0,2,1:T(8,128)(2,1)S(1)} %multiply_convert_fusion) | copy-start | bytes 451588
  81.8 5.0 copy-start.4
  81.8 14.3 %copy-start.12 = (bf16[1,128,512]{2,1,0:T(8,128)(2,1)S(1)}, bf16[1,128,512]{2,1,0:T(8,128)(2,1)}, u32[]{:S(2)}) copy-start(bf16[1,128,512]{2,1,0:T(8,128)(2,1)} %param.15) | copy-start | bytes 393220
  86.8 9.4 %copy-start.11 = (f32[128,256]{1,0:T(8,128)}, f32[128,256]{1,0:T(8,128)S(1)}, u32[]{:S(2)}) copy-start(f32[128,256]{1,0:T(8,128)S(1)} %fusion.37) | copy-start | bytes 393220
  87.1 10.3 %copy-start.10 = (bf16[128,7,84]{0,2,1:T(8,128)(2,1)S(1)}, bf16[128,7,84]{0,2,1:T(8,128)(2,1)}, u32[]{:S(2)}) copy-start(bf16[128,7,84]{0,2,1:T(8,128)(2,1)} %copy-done.9) | copy-start | bytes 451588
  116.7 4.5 copy-start.2
  161.0 4.5 copy-start.2
  197.1 9.4 %copy-start.5 = (bf16[128,12544]{1,0:T(8,128)(2,1)S(1)}, bf16[128,12544]{1,0:T(8,128)(2,1)}, u32[]{:S(2)}) copy-start(bf16[128,12544]{1,0:T(8,128)(2,1)} %copy-done.4) | copy-start | bytes 9633796
  198.4 378.4 %all-to-all-start.2 = ((bf16[2,12,84,256]{3,2,1,0:T(8,128)(2,1)}), bf16[2,12,84,256]{3,2,1,0:T(8,128)(2,1)}, u32[]{:S(2)}, u32[]{:S(2)}) async-start(bf16[2,12,84,256]{3,2,1,0:T(8,128)(2,1)} %bitcast.113), calls=%async_computation.2 | async-start | bytes 2162688 | tf_op jit(solution)/shard_map/all_to_all | solution.py:36
  212.9 353.4 %copy-start.15 = (u32[256]{0:T(256)S(1)}, u32[256]{0:T(256)}, u32[]{:S(2)}) copy-start(u32[256]{0:T(256)} %constant.68) | copy-start | bytes 3076
  547.2 13.8 %collective-permute-start.6 = (f32[104,256]{1,0:T(8,128)S(1)}, f32[104,256]{1,0:T(8,128)S(1)}, u32[]{:S(2)}, u32[]{:S(2)}) collective-permute-start(f32[104,256]{1,0:T(8,128)S(1)} %fusion), channel_id=1, source_target_pairs={{0,14},{2,16},{4,18},{6,20},{8,22},{10,24},{12,26},{14,28},{16,30}... | collective-permute-start | bytes 319496
  549.1 15.3 %collective-permute-start.5 = (f32[104,256]{1,0:T(8,128)S(1)}, f32[104,256]{1,0:T(8,128)S(1)}, u32[]{:S(2)}, u32[]{:S(2)}) collective-permute-start(f32[104,256]{1,0:T(8,128)S(1)} %fusion), channel_id=1, source_target_pairs={{0,12},{2,14},{4,16},{6,18},{8,20},{10,22},{12,24},{14,26},{16,28}... | collective-permute-start | bytes 319496
  551.1 8.0 %collective-permute-start.7 = (f32[34,256]{1,0:T(8,128)S(1)}, f32[34,256]{1,0:T(8,128)S(1)}, u32[]{:S(2)}, u32[]{:S(2)}) collective-permute-start(f32[34,256]{1,0:T(8,128)S(1)} %slice.16), channel_id=1, source_target_pairs={{0,16},{2,18},{4,20},{6,22},{8,24},{10,26},{12,28},{14,30},{16,32}... | collective-permute-start | bytes 104456
  553.0 14.6 %collective-permute-start.4 = (f32[104,256]{1,0:T(8,128)S(1)}, f32[104,256]{1,0:T(8,128)S(1)}, u32[]{:S(2)}, u32[]{:S(2)}) collective-permute-start(f32[104,256]{1,0:T(8,128)S(1)} %fusion), channel_id=1, source_target_pairs={{0,10},{2,12},{4,14},{6,16},{8,18},{10,20},{12,22},{14,24},{16,26}... | collective-permute-start | bytes 319496
  554.9 12.7 %collective-permute-start.3 = (f32[104,256]{1,0:T(8,128)S(1)}, f32[104,256]{1,0:T(8,128)S(1)}, u32[]{:S(2)}, u32[]{:S(2)}) collective-permute-start(f32[104,256]{1,0:T(8,128)S(1)} %fusion), channel_id=1, source_target_pairs={{0,8},{2,10},{4,12},{6,14},{8,16},{10,18},{12,20},{14,22},{16,24},... | collective-permute-start | bytes 319496
  559.1 11.1 %collective-permute-start.2 = (f32[104,256]{1,0:T(8,128)S(1)}, f32[104,256]{1,0:T(8,128)S(1)}, u32[]{:S(2)}, u32[]{:S(2)}) collective-permute-start(f32[104,256]{1,0:T(8,128)S(1)} %fusion), channel_id=1, source_target_pairs={{0,6},{2,8},{4,10},{6,12},{8,14},{10,16},{12,18},{14,20},{16,22},{... | collective-permute-start | bytes 319496
  561.0 11.6 %collective-permute-start.1 = (f32[104,256]{1,0:T(8,128)S(1)}, f32[104,256]{1,0:T(8,128)S(1)}, u32[]{:S(2)}, u32[]{:S(2)}) collective-permute-start(f32[104,256]{1,0:T(8,128)S(1)} %fusion), channel_id=1, source_target_pairs={{0,4},{2,6},{4,8},{6,10},{8,12},{10,14},{12,16},{14,18},{16,20},{1... | collective-permute-start | bytes 319496
  564.4 10.2 %collective-permute-start = (f32[104,256]{1,0:T(8,128)S(1)}, f32[104,256]{1,0:T(8,128)S(1)}, u32[]{:S(2)}, u32[]{:S(2)}) collective-permute-start(f32[104,256]{1,0:T(8,128)S(1)} %fusion), channel_id=1, source_target_pairs={{0,2},{2,4},{4,6},{6,8},{8,10},{10,12},{12,14},{14,16},{16,18},{18... | collective-permute-start | bytes 319496
  580.0 21.7 %copy-start.1 = (bf16[256,512]{1,0:T(8,128)(2,1)S(1)}, bf16[256,512]{1,0:T(8,128)(2,1)}, u32[]{:S(2)}) copy-start(bf16[256,512]{1,0:T(8,128)(2,1)} %param.14) | copy-start | bytes 786436
  (15 other events, 30.5 us)
Sparse Core Ops, SparseCore 0:
  97.5 452.0 all-gather.2
